TPU v7x, 32 devices: a whole 2x2x4 slice. The times are simulated.
32 devices in a mesh: section: 4 (over x, core), seq: 8 (over z, y).
Axes of the slice: x: 2, y: 2, z: 4, core: 2. Of those that a mesh axis runs over, the one named last changes fastest.
Arguments:
- hidden: bfloat16 [2, 1024, 2688], P(None, 'seq'), may hold values from -6 to 6
- lengths: int32 [2], replicated, may hold values from 512 to 1024, as said below
- reward_pos: int32 [2], replicated, may hold values from 384 to 1023, as said below
- in_gain: bfloat16 [2688], P('seq'), may hold values from 0.099609375 to 1.8984375
- w_query: bfloat16 [2688, 2048], P('seq', 'section'), may hold values from -0.077151675 to 0.077151675
- w_key: bfloat16 [2688, 1024], P('seq', 'section'), may hold values from -0.077151675 to 0.077151675
- w_value: bfloat16 [2688, 1024], P('seq', 'section'), may hold values from -0.125 to 0.125
- query_gain: float32 [128], replicated, may hold values from 0.6 to 7
- key_gain: float32 [128], replicated, may hold values from 0.6 to 7
- w_out: bfloat16 [2048, 2688], P('section', 'seq'), may hold values from -0.125 to 0.125
- post_gain: bfloat16 [2688], P('seq'), may hold values from 0.099609375 to 1.8984375
- final_gain: bfloat16 [2688], P('seq'), may hold values from 0.099609375 to 1.8984375
- value_head: bfloat16 [2688], P('seq'), may hold values from -0.125 to 0.125
Outputs:
- token_values: float32 [2, 1024], P(None, 'seq')
- reward: float32 [2], replicated
Inputs may be any that keep to these rules, and one draw needn't show every extreme that they name: `lengths`: in every draw at least one micro-batch has all 1024 tokens valid. reward_pos[m] lies among the last 128 valid tokens of micro-batch m.
All inputs are finite; a program needn't handle non-finite values.
Results may differ from a plain program's by a relative error of at most 0.01.
Values may be sent and summed in bfloat16 or wider, within the bound.
A program may use at most 64 MiB of HBM per device.

v0:
```python
import jax
import jax.numpy as jnp
from jax import lax
from jax.sharding import PartitionSpec as P

HD = 128
GROUP = 2
WINDOW = 1024
norm_eps = 1e-06
query_scale = 168.0 ** (-0.5)
rope_base = 10000.0


def passed_along(array, axis, by):
    devices = lax.axis_size(axis)
    pairs = [(i, i + by) for i in range(devices) if 0 <= i + by < devices]
    return lax.ppermute(array, axis, pairs)


def rms_scale(values, gain_vec):
    return (
        values * lax.rsqrt(jnp.mean(values * values, axis=-1, keepdims=True) + norm_eps) * gain_vec
    )


def rotate_pairs(head_rows, positions):
    half_width = head_rows.shape[-1] // 2
    frequency = rope_base ** (
        -jnp.arange(half_width, dtype=jnp.float32) * 2.0 / head_rows.shape[-1]
    )
    angles = positions.astype(jnp.float32)[:, None] * frequency[None, :]
    target = (angles.shape[0],) + (1,) * (head_rows.ndim - 2) + (half_width,)
    cosine = jnp.cos(angles).reshape(target)
    sine_part = jnp.sin(angles).reshape(target)
    front_half = head_rows[..., :half_width]
    back_half = head_rows[..., half_width:]
    return jnp.concatenate(
        [front_half * cosine - back_half * sine_part, back_half * cosine + front_half * sine_part],
        axis=-1,
    )


def window_blocks(packed, tok_dev):
    block_count = WINDOW // tok_dev + 1
    blocks_held = [packed]
    for offset in range(1, block_count):
        blocks_held.append(passed_along(packed, "seq", offset))
    return jnp.concatenate(blocks_held[::-1], axis=1)


def window_attention(queries, keys_all, values_all, query_pos, key_pos):
    scores = jnp.einsum("qhgd,khd->hgqk", queries, keys_all, preferred_element_type=jnp.float32)
    allowed = (
        (key_pos[None, :] <= query_pos[:, None])
        & (key_pos[None, :] > query_pos[:, None] - WINDOW)
        & (key_pos[None, :] >= 0)
    )
    scores = jnp.where(allowed[None, None], scores, -1e30)
    row_top = jnp.max(scores, axis=-1, keepdims=True)
    exponent = jnp.exp(scores - row_top)
    attn_weights = (exponent / jnp.sum(exponent, axis=-1, keepdims=True)).astype(jnp.bfloat16)
    mixed_heads = jnp.einsum(
        "hgqk,khd->qhgd", attn_weights, values_all, preferred_element_type=jnp.float32
    )
    return mixed_heads.astype(jnp.bfloat16)


def local(
    hidden,
    lengths,
    reward_pos,
    in_gain,
    w_query,
    w_key,
    w_value,
    query_gain,
    key_gain,
    w_out,
    post_gain,
    final_gain,
    value_head,
):
    micro_count, tok_dev, width = hidden.shape
    row_count = micro_count * tok_dev
    qwidth = w_query.shape[1]
    kwidth = w_key.shape[1]
    heads_here = kwidth // HD
    widened = hidden.reshape(row_count, width).astype(jnp.float32)
    inverse = lax.rsqrt(jnp.mean(widened * widened, axis=-1, keepdims=True) + norm_eps)
    seq_pos = lax.axis_index("seq") * tok_dev + jnp.arange(tok_dev, dtype=jnp.int32)
    positions = jnp.tile(seq_pos, micro_count)
    gain_piece = lax.all_gather(in_gain, "seq", axis=0, tiled=True)
    query_piece = lax.all_gather(w_query, "seq", axis=0, tiled=True)
    key_piece = lax.all_gather(w_key, "seq", axis=0, tiled=True)
    value_piece = lax.all_gather(w_value, "seq", axis=0, tiled=True)
    post_piece = lax.all_gather(post_gain, "seq", axis=0, tiled=True)
    final_piece = lax.all_gather(final_gain, "seq", axis=0, tiled=True)
    head_piece = lax.all_gather(value_head, "seq", axis=0, tiled=True)
    normed = (widened * inverse * gain_piece.astype(jnp.float32)).astype(jnp.bfloat16)
    query_acc = jnp.dot(normed, query_piece, preferred_element_type=jnp.float32)
    key_acc = jnp.dot(normed, key_piece, preferred_element_type=jnp.float32)
    value_acc = jnp.dot(normed, value_piece, preferred_element_type=jnp.float32)
    post_full = post_piece.astype(jnp.float32)
    final_full = final_piece.astype(jnp.float32)
    head_full = head_piece.astype(jnp.float32)
    folded = (query_acc, key_acc, value_acc, post_full, final_full, head_full)
    queries = folded[0].reshape(row_count, heads_here, GROUP, HD)
    queries = (rotate_pairs(rms_scale(queries, query_gain), positions) * query_scale).astype(
        jnp.bfloat16
    )
    keys_new = folded[1].reshape(row_count, heads_here, HD)
    keys_new = (
        rotate_pairs(rms_scale(keys_new, key_gain), positions)
        .astype(jnp.bfloat16)
        .reshape(row_count, kwidth)
    )
    vals_new = folded[2].astype(jnp.bfloat16)
    packed = jnp.concatenate([keys_new, vals_new], axis=1).reshape(micro_count, tok_dev, 2 * kwidth)
    window_rows = window_blocks(packed, tok_dev)
    key_pos = seq_pos[0] - WINDOW + jnp.arange(WINDOW + tok_dev, dtype=jnp.int32)
    mixed_list = []
    for micro_id in range(micro_count):
        block_queries = queries[micro_id * tok_dev : (micro_id + 1) * tok_dev]
        keys_all = window_rows[micro_id, :, :kwidth].reshape(-1, heads_here, HD)
        values_all = window_rows[micro_id, :, kwidth:].reshape(-1, heads_here, HD)
        mixed_list.append(
            window_attention(block_queries, keys_all, values_all, seq_pos, key_pos).reshape(
                tok_dev, qwidth
            )
        )
    mixed_all = jnp.concatenate(mixed_list, axis=0)
    branch = jnp.dot(
        mixed_all,
        lax.all_gather(w_out, "seq", axis=1, tiled=True),
        preferred_element_type=jnp.float32,
    )
    post_full, final_full, head_full = (folded[3], folded[4], folded[5])
    share_width = width // lax.axis_size("section")
    offset = lax.axis_index("section") * share_width
    share = lax.psum_scatter(branch, "section", scatter_dimension=1, tiled=True)
    branch_sq = lax.psum(jnp.sum(share * share, axis=1), "section")
    share_scale = lax.rsqrt(branch_sq / width + norm_eps)[:, None]
    post_share = lax.dynamic_slice_in_dim(post_full, offset, share_width, 0)
    updated = (
        lax.dynamic_slice_in_dim(widened, offset, share_width, 1) + share * share_scale * post_share
    ).astype(jnp.bfloat16)
    updated_wide = updated.astype(jnp.float32)
    residual_sq = lax.psum(jnp.sum(updated_wide * updated_wide, axis=1), "section")
    final_share = lax.dynamic_slice_in_dim(final_full, offset, share_width, 0)
    last_rows = (
        updated_wide * lax.rsqrt(residual_sq / width + norm_eps)[:, None] * final_share
    ).astype(jnp.bfloat16)
    head_share = lax.dynamic_slice_in_dim(head_full, offset, share_width, 0).astype(jnp.bfloat16)
    raw_values = lax.psum(
        jnp.dot(last_rows, head_share, preferred_element_type=jnp.float32), "section"
    )
    raw_values = raw_values.reshape(micro_count, tok_dev)
    token_values = jnp.where(seq_pos[None, :] < lengths[:, None], raw_values, 0.0)
    partial_value = jnp.sum(
        jnp.where(seq_pos[None, :] == reward_pos[:, None], token_values, 0.0), axis=1
    )
    reward = lax.psum(partial_value, "seq")
    return (token_values, reward)


def solution(mesh):
    placed = (
        P(None, "seq", None),
        P(),
        P(),
        P("seq"),
        P("seq", "section"),
        P("seq", "section"),
        P("seq", "section"),
        P(),
        P(),
        P("section", "seq"),
        P("seq"),
        P("seq"),
        P("seq"),
    )
    return jax.shard_map(
        local, mesh=mesh, in_specs=placed, out_specs=(P(None, "seq"), P()), check_vma=False
    )
```

profile of v0, /device:TPU:0, one launch (start us, length us, event | category | flops | bytes accessed | tf_op | source)
XLA Modules:
  0.0 331.5 jit_solution(10913897586998984354)
XLA Ops:
  15.5 39.5 %all-reduce.4 = (bf16[2688]{0:T(1024)(128)(2,1)S(1)}, bf16[2688]{0:T(1024)(128)(2,1)S(1)}, bf16[2688]{0:T(1024)(128)(2,1)S(1)}, bf16[2688]{0:T(1024)(128)(2,1)S(1)}) all-reduce(bf16[2688]{0:T(1024)(128)(2,1)S(1)} %dynamic-update-slice.3, bf16[2688]{0:T(1024)(128)(2,1)S(1)} %dynamic-update-slice, ...), channel_id=1, replica_groups=mesh['section'=4,'seq'=8] {'seq'}, use_global_device_ids=true, to_apply=%add.3 | all-reduce | flops 10752 | bytes 43008
  55.1 1.7 multiply_reduce_fusion
  56.8 1.7 copy.43
  58.4 2.9 multiply_convert_fusion.1
  61.7 2.6 copy.24
  64.3 2.4 multiply_reduce_fusion.3
  66.9 31.5 %all-gather.7.cloned.1.call-done = bf16[2688,256]{1,0:T(8,128)(2,1)} async-done(((bf16[336,256]{1,0:T(8,128)(2,1)}), bf16[2688,256]{1,0:T(8,128)(2,1)}) %all-gather.7.cloned.1.call-update) | async-done | bytes 1376272 | tf_op jit(solution)/shard_map/all_gather | solution.py:95
  98.4 2.4 fusion.15
  101.6 4.0 %collective-permute-start.1 = (bf16[2,128,512]{1,2,0:T(8,128)(2,1)S(1)}, bf16[2,128,512]{1,2,0:T(8,128)(2,1)S(1)}, u32[]{:S(2)}, u32[]{:S(2)}) collective-permute-start(bf16[2,128,512]{1,2,0:T(8,128)(2,1)S(1)} %pad_maximum_fusion), channel_id=1, source_target_pairs={{0,7},{8,15},{16,23},{24,31}} | collective-permute-start | bytes 786440 | tf_op jit(solution)/shard_map/ppermute | solution.py:17
  106.9 1.5 and_and_fusion
  111.0 2.4 collective-permute-start.5
  113.6 2.9 collective-permute-done.1
  117.8 9.9 %collective-permute-done.2 = bf16[2,128,512]{1,2,0:T(8,128)(2,1)S(1)} collective-permute-done((bf16[2,128,512]{1,2,0:T(8,128)(2,1)S(1)}, bf16[2,128,512]{1,2,0:T(8,128)(2,1)S(1)}, u32[]{:S(2)}, u32[]{:S(2)}) %collective-permute-start.2) | collective-permute-done | bytes 262176 | tf_op jit(solution)/shard_map/ppermute | solution.py:17
  127.7 1.5 collective-permute-start.7
  129.2 5.3 %collective-permute-done.3 = bf16[2,128,512]{1,2,0:T(8,128)(2,1)S(1)} collective-permute-done((bf16[2,128,512]{1,2,0:T(8,128)(2,1)S(1)}, bf16[2,128,512]{1,2,0:T(8,128)(2,1)S(1)}, u32[]{:S(2)}, u32[]{:S(2)}) %collective-permute-start.3) | collective-permute-done | bytes 262176 | tf_op jit(solution)/shard_map/ppermute | solution.py:17
  134.6 5.6 %collective-permute-done.4 = bf16[2,128,512]{1,2,0:T(8,128)(2,1)S(1)} collective-permute-done((bf16[2,128,512]{1,2,0:T(8,128)(2,1)S(1)}, bf16[2,128,512]{1,2,0:T(8,128)(2,1)S(1)}, u32[]{:S(2)}, u32[]{:S(2)}) %collective-permute-start.4) | collective-permute-done | bytes 262176 | tf_op jit(solution)/shard_map/ppermute | solution.py:17
  140.3 5.6 %collective-permute-done.5 = bf16[2,128,512]{1,2,0:T(8,128)(2,1)S(1)} collective-permute-done((bf16[2,128,512]{1,2,0:T(8,128)(2,1)S(1)}, bf16[2,128,512]{1,2,0:T(8,128)(2,1)S(1)}, u32[]{:S(2)}, u32[]{:S(2)}) %collective-permute-start.5) | collective-permute-done | bytes 262176 | tf_op jit(solution)/shard_map/ppermute | solution.py:17
  145.9 3.4 %collective-permute-done.6 = bf16[2,128,512]{1,2,0:T(8,128)(2,1)S(1)} collective-permute-done((bf16[2,128,512]{1,2,0:T(8,128)(2,1)S(1)}, bf16[2,128,512]{1,2,0:T(8,128)(2,1)S(1)}, u32[]{:S(2)}, u32[]{:S(2)}) %collective-permute-start.6) | collective-permute-done | bytes 262176 | tf_op jit(solution)/shard_map/ppermute | solution.py:17
  150.8 27.7 %all-gather.9.cloned.1.call-done = bf16[2688,512]{1,0:T(8,128)(2,1)} async-done(((bf16[336,512]{1,0:T(8,128)(2,1)}), bf16[2688,512]{1,0:T(8,128)(2,1)}) %all-gather.9.cloned.1.call-update) | async-done | bytes 2752528 | tf_op jit(solution)/shard_map/all_gather | solution.py:93
  178.5 4.5 %copy.27 = bf16[512,2688]{1,0:T(8,128)(2,1)} copy(bf16[512,2688]{0,1:T(8,128)(2,1)} %bitcast.94) | data formatting | bytes 5505024 | tf_op jit(solution)/shard_map/dot_general | solution.py:100
  183.0 3.2 multiply_reduce_fusion.2
  187.1 2.1 fusion.64
  189.2 1.8 fusion.61
  191.1 3.2 fusion.14
  194.3 3.1 fusion.13
  197.3 46.1 %all-gather.11.cloned.1.call-done = bf16[512,2688]{0,1:T(8,128)(2,1)} async-done(((bf16[512,336]{0,1:T(8,128)(2,1)}), bf16[512,2688]{0,1:T(8,128)(2,1)}) %all-gather.11.cloned.1.call-update) | async-done | bytes 2752528 | tf_op jit(solution)/shard_map/all_gather | solution.py:134
  243.4 4.3 %fusion.24 = f32[256,2688]{0,1:T(8,128)} fusion(bf16[512,2688]{0,1:T(8,128)(2,1)} %all-gather.11.cloned.1.call-done, bf16[128,512]{0,1:T(8,128)(2,1)} %bitcast.108, bf16[128,512]{0,1:T(8,128)(2,1)} %bitcast.107), kind=kOutput, calls=%fused_computation.39 | convolution fusion | flops 705167360 | bytes 5767168 | tf_op jit(solution)/shard_map/dot_general | solution.py:132
  248.0 33.8 %reduce-scatter.2.cloned.1.call-done = f32[256,672]{0,1:T(8,128)} async-done(((f32[256,2688]{0,1:T(8,128)}), f32[256,672]{0,1:T(8,128)}) %reduce-scatter.2.cloned.1.call-update) | async-done | bytes 688144 | tf_op jit(solution)/shard_map/reduce_scatter | solution.py:140
  283.0 5.8 %psum.28 = f32[256]{0:T(256)S(1)} all-reduce(f32[256]{0:T(256)S(1)} %multiply_reduce_fusion.1), channel_id=1, replica_groups=mesh['section'=4,'seq'=8] {'section'}, use_global_device_ids=true, to_apply=%region_9.10 | all-reduce | flops 256 | bytes 2048 | tf_op jit(solution)/shard_map/psum | solution.py:141
  290.1 5.7 %psum.29 = f32[256]{0:T(256)S(1)} all-reduce(f32[256]{0:T(256)S(1)} %get-tuple-element.8), channel_id=1, replica_groups=mesh['section'=4,'seq'=8] {'section'}, use_global_device_ids=true, to_apply=%region_11.12 | all-reduce | flops 256 | bytes 2048 | tf_op jit(solution)/shard_map/psum | solution.py:148
  296.0 6.3 %psum.30 = f32[2,128]{1,0:T(2,128)S(1)} all-reduce(f32[2,128]{1,0:T(2,128)S(1)} %bitcast.110), channel_id=1, replica_groups=mesh['section'=4,'seq'=8] {'section'}, use_global_device_ids=true, to_apply=%region_12.13 | all-reduce | flops 256 | bytes 2048 | tf_op jit(solution)/shard_map/psum | solution.py:154
  303.1 21.9 %psum.31 = f32[2]{0:T(128)} all-reduce(f32[2]{0:T(128)S(1)} %get-tuple-element.6), channel_id=1, replica_groups=mesh['section'=4,'seq'=8] {'seq'}, use_global_device_ids=true, to_apply=%region_14.15 | all-reduce | flops 2 | bytes 16 | tf_op jit(solution)/shard_map/psum | solution.py:162
  (78 shorter events, 20.7 us)
Async XLA Ops:
  7.2 54.5 %all-gather.5.cloned.1.call-start = ((), (), s32[]{:S(2)}) async-start(), calls=%async_computation.1 | async-start | bytes 1548288 | tf_op jit(solution)/shard_map/all_gather | solution.py:94
  7.9 90.5 %all-gather.7.cloned.1.call-start = ((), (), s32[]{:S(2)}) async-start(), calls=%async_computation.2 | async-start | bytes 1548288 | tf_op jit(solution)/shard_map/all_gather | solution.py:95
  8.6 169.8 %all-gather.9.cloned.1.call-start = ((), (), s32[]{:S(2)}) async-start(), calls=%async_computation.3 | async-start | bytes 3096576 | tf_op jit(solution)/shard_map/all_gather | solution.py:93
  9.4 234.0 %all-gather.11.cloned.1.call-start = ((), (), s32[]{:S(2)}) async-start(), calls=%async_computation.4 | async-start | bytes 3096576 | tf_op jit(solution)/shard_map/all_gather | solution.py:134
  10.0 271.8 %reduce-scatter.2.cloned.1.call-start = ((), (), s32[]{:S(2)}) async-start(), calls=%async_computation.5 | async-start | bytes 3440640 | tf_op jit(solution)/shard_map/reduce_scatter | solution.py:140
  61.7 5.0 %copy-start.1 = (f32[128]{0:T(128)S(1)}, f32[128]{0:T(128)}, u32[]{:S(2)}) copy-start(f32[128]{0:T(128)} %param.21) | copy-start | bytes 1540
  100.9 10.1 %collective-permute-start = (bf16[2,128,512]{1,2,0:T(8,128)(2,1)S(1)}, bf16[2,128,512]{1,2,0:T(8,128)(2,1)S(1)}, u32[]{:S(2)}, u32[]{:S(2)}) collective-permute-start(bf16[2,128,512]{1,2,0:T(8,128)(2,1)S(1)} %pad_maximum_fusion), channel_id=1, source_target_pairs={} | collective-permute-start | bytes 786440 | tf_op jit(solution)/shard_map/ppermute | solution.py:17
  101.6 14.9 %collective-permute-start.1 = (bf16[2,128,512]{1,2,0:T(8,128)(2,1)S(1)}, bf16[2,128,512]{1,2,0:T(8,128)(2,1)S(1)}, u32[]{:S(2)}, u32[]{:S(2)}) collective-permute-start(bf16[2,128,512]{1,2,0:T(8,128)(2,1)S(1)} %pad_maximum_fusion), channel_id=1, source_target_pairs={{0,7},{8,15},{16,23},{24,31}} | collective-permute-start | bytes 786440 | tf_op jit(solution)/shard_map/ppermute | solution.py:17
  105.6 22.1 %collective-permute-start.2 = (bf16[2,128,512]{1,2,0:T(8,128)(2,1)S(1)}, bf16[2,128,512]{1,2,0:T(8,128)(2,1)S(1)}, u32[]{:S(2)}, u32[]{:S(2)}) collective-permute-start(bf16[2,128,512]{1,2,0:T(8,128)(2,1)S(1)} %pad_maximum_fusion), channel_id=1, source_target_pairs={{0,6},{1,7},{8,14},{9,15},{16,22},{17,23},{24,30},{25,31}} | collective-permute-start | bytes 786440 | tf_op jit(solution)/shard_map/ppermute | solution.py:17
  108.4 26.2 %collective-permute-start.3 = (bf16[2,128,512]{1,2,0:T(8,128)(2,1)S(1)}, bf16[2,128,512]{1,2,0:T(8,128)(2,1)S(1)}, u32[]{:S(2)}, u32[]{:S(2)}) collective-permute-start(bf16[2,128,512]{1,2,0:T(8,128)(2,1)S(1)} %pad_maximum_fusion), channel_id=1, source_target_pairs={{0,5},{1,6},{2,7},{8,13},{9,14},{10,15},{16,21},{17,22},{18,23},{2... | collective-permute-start | bytes 786440 | tf_op jit(solution)/shard_map/ppermute | solution.py:17
  109.7 30.5 %collective-permute-start.4 = (bf16[2,128,512]{1,2,0:T(8,128)(2,1)S(1)}, bf16[2,128,512]{1,2,0:T(8,128)(2,1)S(1)}, u32[]{:S(2)}, u32[]{:S(2)}) collective-permute-start(bf16[2,128,512]{1,2,0:T(8,128)(2,1)S(1)} %pad_maximum_fusion), channel_id=1, source_target_pairs={{0,4},{1,5},{2,6},{3,7},{8,12},{9,13},{10,14},{11,15},{16,20},{17,... | collective-permute-start | bytes 786440 | tf_op jit(solution)/shard_map/ppermute | solution.py:17
  111.0 34.8 %collective-permute-start.5 = (bf16[2,128,512]{1,2,0:T(8,128)(2,1)S(1)}, bf16[2,128,512]{1,2,0:T(8,128)(2,1)S(1)}, u32[]{:S(2)}, u32[]{:S(2)}) collective-permute-start(bf16[2,128,512]{1,2,0:T(8,128)(2,1)S(1)} %pad_maximum_fusion), channel_id=1, source_target_pairs={{0,3},{1,4},{2,5},{3,6},{4,7},{8,11},{9,12},{10,13},{11,14},{12,15... | collective-permute-start | bytes 786440 | tf_op jit(solution)/shard_map/ppermute | solution.py:17
  116.5 32.9 %collective-permute-start.6 = (bf16[2,128,512]{1,2,0:T(8,128)(2,1)S(1)}, bf16[2,128,512]{1,2,0:T(8,128)(2,1)S(1)}, u32[]{:S(2)}, u32[]{:S(2)}) collective-permute-start(bf16[2,128,512]{1,2,0:T(8,128)(2,1)S(1)} %pad_maximum_fusion), channel_id=1, source_target_pairs={{0,2},{1,3},{2,4},{3,5},{4,6},{5,7},{8,10},{9,11},{10,12},{11,13},... | collective-permute-start | bytes 786440 | tf_op jit(solution)/shard_map/ppermute | solution.py:17
  127.7 21.7 %collective-permute-start.7 = (bf16[2,128,512]{1,2,0:T(8,128)(2,1)S(1)}, bf16[2,128,512]{1,2,0:T(8,128)(2,1)S(1)}, u32[]{:S(2)}, u32[]{:S(2)}) collective-permute-start(bf16[2,128,512]{1,2,0:T(8,128)(2,1)S(1)} %pad_maximum_fusion), channel_id=1, source_target_pairs={{0,1},{1,2},{2,3},{3,4},{4,5},{5,6},{6,7},{8,9},{9,10},{10,11},{11... | collective-permute-start | bytes 786440 | tf_op jit(solution)/shard_map/ppermute | solution.py:17
  183.0 3.2 copy-start.2
  186.4 2.9 copy-start
  247.7 54.6 %copy-start.3 = (s32[2]{0:T(128)S(1)}, s32[2]{0:T(128)}, u32[]{:S(2)}) copy-start(s32[2]{0:T(128)} %param.15) | copy-start | bytes 28
  247.7 54.6 %copy-start.4 = (s32[2]{0:T(128)S(1)}, s32[2]{0:T(128)}, u32[]{:S(2)}) copy-start(s32[2]{0:T(128)} %param.14) | copy-start | bytes 28
Sparse Core Ops, SparseCore 0:
  10.2 45.0 all-gather.4
  57.4 40.9 all-gather.6
  100.6 77.8 all-gather.8
  180.5 62.8 all-gather.10
  247.9 33.8 reduce-scatter.1
where the time goes:
time: 332 us; the launch traced here: 331 us
  waiting for transfers between devices  174 us (52%)
  blocking collectives  79.1 us (24%)
  matrix products  22.7 us (7%)
  local copies, waits for them, and re-layouts  15.4 us (5%)
  between operations  14.8 us (4%)
  starting transfers between devices  14 us (4%)
  other arithmetic  11.1 us (3%)
    all_gather x1, waiting for transfers between devices, local(): lax.all_gather(w_out, 'seq', axis=1, tiled=True)  46.1 us
    unnamed x1, blocking collectives  39.5 us
    reduce_scatter x1, waiting for transfers between devices, local(): share = lax.psum_scatter(branch, 'section', scatter_dimension=1, tiled=True)  33.8 us
    ppermute x8, waiting for transfers between devices, passed_along(): return lax.ppermute(array, axis, pairs)  32.7 us
    all_gather x1, waiting for transfers between devices, local(): value_piece = lax.all_gather(w_value, 'seq', axis=0, tiled=True)  31.5 us
    all_gather x1, waiting for transfers between devices, local(): query_piece = lax.all_gather(w_query, 'seq', axis=0, tiled=True)  27.7 us
    psum x1, blocking collectives, local(): reward = lax.psum(partial_value, 'seq')  21.9 us
    ppermute x8, starting transfers between devices, passed_along(): return lax.ppermute(array, axis, pairs)  13.8 us
  transfers between devices with their start and end apart: 13, of which 10 were waited for; matrix products, arithmetic and copies ran while one was open for 12% of the time, Pallas kernels for 0%

commit v1 on v0

--- a/solution.py
+++ b/solution.py
@@ -90,7 +90,12 @@
     seq_pos = lax.axis_index("seq") * tok_dev + jnp.arange(tok_dev, dtype=jnp.int32)
     positions = jnp.tile(seq_pos, micro_count)
     gain_piece = lax.all_gather(in_gain, "seq", axis=0, tiled=True)
-    query_piece = lax.all_gather(w_query, "seq", axis=0, tiled=True)
+    ring = [w_query]
+    for hop in range(7):
+        ring.append(lax.ppermute(ring[-1], "seq", [(dev, (dev + 1) % 8) for dev in range(8)]))
+    query_piece = jnp.roll(
+        jnp.concatenate(ring[::-1], axis=0), (lax.axis_index("seq") + 1) * ring[0].shape[0], axis=0
+    )
     key_piece = lax.all_gather(w_key, "seq", axis=0, tiled=True)
     value_piece = lax.all_gather(w_value, "seq", axis=0, tiled=True)
     post_piece = lax.all_gather(post_gain, "seq", axis=0, tiled=True)

time: 332 us -> 306 us (0.922)
  waiting for transfers between devices: 174 us -> 117 us
  local copies, waits for them, and re-layouts: 15.4 us -> 35.3 us
  starting transfers between devices: 14 us -> 23.1 us
  other arithmetic: 11.1 us -> 14.6 us
    ppermute x0 -> x7, waiting for transfers between devices: none -> 57.1 us  [local(): lax.ppermute(ring[-1], 'seq', [(dev, (dev + 1) % 8) for dev in range(8)])]
    all_gather x1, waiting for transfers between devices: 46.1 us -> 0.01 us  [local(): lax.all_gather(w_out, 'seq', axis=1, tiled=True)]
    all_gather x1, waiting for transfers between devices: 31.5 us -> 0.01 us  [local(): value_piece = lax.all_gather(w_value, 'seq', axis=0, tiled=True)]
    all_gather x1 -> x0, waiting for transfers between devices: 27.7 us -> none  [local(): query_piece = lax.all_gather(w_query, 'seq', axis=0, tiled=True)]
    ppermute x8, waiting for transfers between devices: 32.7 us -> 9.54 us  [passed_along(): return lax.ppermute(array, axis, pairs)]
    reduce_scatter x1, waiting for transfers between devices: 33.8 us -> 49 us  [local(): share = lax.psum_scatter(branch, 'section', scatter_dimension=1, tiled=True)]
    unnamed x27 -> x58, local copies, waits for them, and re-layouts: 5.26 us -> 18.2 us
    ppermute x8, starting transfers between devices: 13.8 us -> 19.8 us  [passed_along(): return lax.ppermute(array, axis, pairs)]
  transfers between devices with their start and end apart: 13 -> 19, of which waited for: 10 -> 8; matrix products, arithmetic and copies ran while one was open for 12% -> 21% of each run, Pallas kernels for 0% -> 0%
where the time goes in v1:
time: 306 us; the launch traced here: 305 us
  waiting for transfers between devices  117 us (38%)
  blocking collectives  76.7 us (25%)
  local copies, waits for them, and re-layouts  35.3 us (12%)
  matrix products  23.2 us (8%)
  starting transfers between devices  23.1 us (8%)
  between operations  14.9 us (5%)
  other arithmetic  14.6 us (5%)
    ppermute x7, waiting for transfers between devices, local(): lax.ppermute(ring[-1], 'seq', [(dev, (dev + 1) % 8) for dev in range(8)])  57.1 us
    reduce_scatter x1, waiting for transfers between devices, local(): share = lax.psum_scatter(branch, 'section', scatter_dimension=1, tiled=True)  49 us
    unnamed x1, blocking collectives  37.2 us
    psum x1, blocking collectives, local(): reward = lax.psum(partial_value, 'seq')  21.9 us
    ppermute x8, starting transfers between devices, passed_along(): return lax.ppermute(array, axis, pairs)  19.8 us
    unnamed x58, local copies, waits for them, and re-layouts  18.2 us
    ppermute x8, waiting for transfers between devices, passed_along(): return lax.ppermute(array, axis, pairs)  9.54 us
    dot_general x2, local copies, waits for them, and re-layouts, local(): query_acc = jnp.dot(normed, query_piece, preferred_element_type=jnp.float32)  6.72 us
  transfers between devices with their start and end apart: 19, of which 8 were waited for; matrix products, arithmetic and copies ran while one was open for 21% of the time, Pallas kernels for 0%

profile of v1, /device:TPU:0, one launch (start us, length us, event | category | flops | bytes accessed | tf_op | source)
XLA Modules:
  0.0 304.9 jit_solution(17635762349784366831)
XLA Ops:
  8.7 3.0 collective-permute-start.8
  17.2 37.2 %all-reduce.4 = (bf16[2688]{0:T(1024)(128)(2,1)}, bf16[2688]{0:T(1024)(128)(2,1)S(1)}, bf16[2688]{0:T(1024)(128)(2,1)S(1)}, bf16[2688]{0:T(1024)(128)(2,1)S(1)}) all-reduce(bf16[2688]{0:T(1024)(128)(2,1)S(1)} %dynamic-update-slice.3, bf16[2688]{0:T(1024)(128)(2,1)S(1)} %dynamic-update-slice, ...), channel_id=1, replica_groups=mesh['section'=4,'seq'=8] {'seq'}, use_global_device_ids=true, to_apply=%add.3 | all-reduce | flops 10752 | bytes 43008
  54.5 1.7 multiply_reduce_fusion
  56.2 8.2 %collective-permute-done.9 = bf16[336,512]{1,0:T(8,128)(2,1)S(1)} collective-permute-done((bf16[336,512]{1,0:T(8,128)(2,1)S(1)}, bf16[336,512]{1,0:T(8,128)(2,1)S(1)}, u32[]{:S(2)}, u32[]{:S(2)}) %collective-permute-start.9) | collective-permute-done | bytes 344096 | tf_op jit(solution)/shard_map/ppermute | solution.py:95
  66.0 13.1 %collective-permute-done.10 = bf16[336,512]{1,0:T(8,128)(2,1)S(1)} collective-permute-done((bf16[336,512]{1,0:T(8,128)(2,1)S(1)}, bf16[336,512]{1,0:T(8,128)(2,1)S(1)}, u32[]{:S(2)}, u32[]{:S(2)}) %collective-permute-start.10) | collective-permute-done | bytes 344096 | tf_op jit(solution)/shard_map/ppermute | solution.py:95
  79.1 10.0 %collective-permute-done.11 = bf16[336,512]{1,0:T(8,128)(2,1)} collective-permute-done((bf16[336,512]{1,0:T(8,128)(2,1)S(1)}, bf16[336,512]{1,0:T(8,128)(2,1)}, u32[]{:S(2)}, u32[]{:S(2)}) %collective-permute-start.11) | collective-permute-done | bytes 344096 | tf_op jit(solution)/shard_map/ppermute | solution.py:95
  92.9 13.5 %collective-permute-done.12 = bf16[336,512]{1,0:T(8,128)(2,1)} collective-permute-done((bf16[336,512]{1,0:T(8,128)(2,1)}, bf16[336,512]{1,0:T(8,128)(2,1)}, u32[]{:S(2)}, u32[]{:S(2)}) %collective-permute-start.12) | collective-permute-done | bytes 344096 | tf_op jit(solution)/shard_map/ppermute | solution.py:95
  107.9 12.3 %collective-permute-done.13 = bf16[336,512]{1,0:T(8,128)(2,1)} collective-permute-done((bf16[336,512]{1,0:T(8,128)(2,1)}, bf16[336,512]{1,0:T(8,128)(2,1)}, u32[]{:S(2)}, u32[]{:S(2)}) %collective-permute-start.13) | collective-permute-done | bytes 344096 | tf_op jit(solution)/shard_map/ppermute | solution.py:95
  120.2 2.5 copy.24
  122.8 2.4 multiply_reduce_fusion.3
  129.1 3.0 fusion.15
  132.2 1.7 copy.26
  133.8 1.7 pad_maximum_fusion
  137.1 7.4 %collective-permute-start.1 = (bf16[2,128,512]{1,2,0:T(8,128)(2,1)}, bf16[2,128,512]{1,2,0:T(8,128)(2,1)}, u32[]{:S(2)}, u32[]{:S(2)}) collective-permute-start(bf16[2,128,512]{1,2,0:T(8,128)(2,1)} %pad_maximum_fusion), channel_id=1, source_target_pairs={{0,7},{8,15},{16,23},{24,31}} | collective-permute-start | bytes 786440 | tf_op jit(solution)/shard_map/ppermute | solution.py:17
  144.4 2.0 collective-permute-start.2
  146.5 2.0 collective-permute-start.3
  148.5 2.0 collective-permute-start.4
  158.8 2.2 dynamic-slice_bitcast_fusion
  161.0 4.5 %copy.27 = bf16[512,2688]{1,0:T(8,128)(2,1)} copy(bf16[512,2688]{0,1:T(8,128)(2,1)} %dynamic-slice_bitcast_fusion) | data formatting | bytes 5505024 | tf_op jit(solution)/shard_map/dot_general | solution.py:105
  165.5 3.2 %multiply_reduce_fusion.2 = (f32[256,2,2]{0,2,1:T(2,128)S(1)}, f32[256,2,2,128]{0,3,2,1:T(8,128)S(1)}) fusion(bf16[256,2688,1,1]{1,0,3,2:T(8,128)(2,1)} %bitcast.97, bf16[2,2,128,2688]{3,2,1,0:T(8,128)(2,1)} %bitcast.95), kind=kOutput, calls=%fused_computation.35 | convolution fusion | flops 704904192 | bytes 4657152 | tf_op jit(solution)/shard_map/dot_general | solution.py:105
  174.4 2.3 collective-permute-start.7
  181.0 8.4 %collective-permute-done.6 = bf16[2,128,512]{1,2,0:T(8,128)(2,1)S(1)} collective-permute-done((bf16[2,128,512]{1,2,0:T(8,128)(2,1)}, bf16[2,128,512]{1,2,0:T(8,128)(2,1)S(1)}, u32[]{:S(2)}, u32[]{:S(2)}) %collective-permute-start.6) | collective-permute-done | bytes 262176 | tf_op jit(solution)/shard_map/ppermute | solution.py:17
  190.9 2.0 fusion.64
  192.9 1.8 fusion.61
  194.7 3.2 %fusion.14 = bf16[2,128,2,128]{3,1,2,0:T(8,128)(2,1)} fusion(bf16[1152,2,128,1]{0,2,3,1:T(8,128)(2,1)} %bitcast.105, f32[2,2,128]{2,1,0:T(2,128)S(1)} %fusion.64, bf16[1152,2,128,1]{0,2,3,1:T(8,128)(2,1)} %bitcast.104, pred[128,1152]{0,1:T(8,128)(4,1)S(1)} %copy-done.8, bf16[256,2,2,128]{0,3,2,1:T(8,128)(2,1)} %fusion.19), kind=kOutput, calls=%fused_computation.22 | convolution fusion | flops 304416384 | bytes 1591296 | tf_op jit(solution)/shard_map/hgqk,khd->qhgd/dot_general | solution.py:62
  197.9 3.0 fusion.13
  200.9 4.3 %fusion.24 = f32[256,2688]{0,1:T(8,128)} fusion(bf16[512,2688]{0,1:T(8,128)(2,1)} %all-gather.8.cloned.1.call-done, bf16[128,512]{0,1:T(8,128)(2,1)} %bitcast.108, bf16[128,512]{0,1:T(8,128)(2,1)} %bitcast.107), kind=kOutput, calls=%fused_computation.40 | convolution fusion | flops 705167360 | bytes 5767168 | tf_op jit(solution)/shard_map/dot_general | solution.py:137
  206.2 49.0 %reduce-scatter.2.cloned.1.call-done = f32[256,672]{0,1:T(8,128)} async-done(((f32[256,2688]{0,1:T(8,128)}), f32[256,672]{0,1:T(8,128)}) %reduce-scatter.2.cloned.1.call-update) | async-done | bytes 688144 | tf_op jit(solution)/shard_map/reduce_scatter | solution.py:145
  256.4 5.8 %psum.28 = f32[256]{0:T(256)S(1)} all-reduce(f32[256]{0:T(256)S(1)} %multiply_reduce_fusion.1), channel_id=1, replica_groups=mesh['section'=4,'seq'=8] {'section'}, use_global_device_ids=true, to_apply=%region_9.10 | all-reduce | flops 256 | bytes 2048 | tf_op jit(solution)/shard_map/psum | solution.py:146
  263.5 5.7 %psum.29 = f32[256]{0:T(256)S(1)} all-reduce(f32[256]{0:T(256)S(1)} %get-tuple-element.8), channel_id=1, replica_groups=mesh['section'=4,'seq'=8] {'section'}, use_global_device_ids=true, to_apply=%region_11.12 | all-reduce | flops 256 | bytes 2048 | tf_op jit(solution)/shard_map/psum | solution.py:153
  269.4 6.3 %psum.30 = f32[2,128]{1,0:T(2,128)S(1)} all-reduce(f32[2,128]{1,0:T(2,128)S(1)} %bitcast.110), channel_id=1, replica_groups=mesh['section'=4,'seq'=8] {'section'}, use_global_device_ids=true, to_apply=%region_12.13 | all-reduce | flops 256 | bytes 2048 | tf_op jit(solution)/shard_map/psum | solution.py:159
  276.5 21.9 %psum.31 = f32[2]{0:T(128)} all-reduce(f32[2]{0:T(128)S(1)} %get-tuple-element.6), channel_id=1, replica_groups=mesh['section'=4,'seq'=8] {'seq'}, use_global_device_ids=true, to_apply=%region_14.15 | all-reduce | flops 2 | bytes 16 | tf_op jit(solution)/shard_map/psum | solution.py:167
  (122 shorter events, 42.7 us)
Async XLA Ops:
  7.2 57.3 %copy-start = (bf16[2,128,2688]{2,1,0:T(8,128)(2,1)S(1)}, bf16[2,128,2688]{2,1,0:T(8,128)(2,1)}, u32[]{:S(2)}) copy-start(bf16[2,128,2688]{2,1,0:T(8,128)(2,1)} %param.13) | copy-start | bytes 4128772
  7.2 113.0 %all-gather.4.cloned.1.call-start = ((), (), s32[]{:S(2)}) async-start(), calls=%async_computation.1 | async-start | bytes 1548288 | tf_op jit(solution)/shard_map/all_gather | solution.py:99
  7.9 121.2 %all-gather.6.cloned.1.call-start = ((), (), s32[]{:S(2)}) async-start(), calls=%async_computation.2 | async-start | bytes 1548288 | tf_op jit(solution)/shard_map/all_gather | solution.py:100
  8.7 192.3 %all-gather.8.cloned.1.call-start = ((), (), s32[]{:S(2)}) async-start(), calls=%async_computation.3 | async-start | bytes 3096576 | tf_op jit(solution)/shard_map/all_gather | solution.py:139
  8.7 45.7 %collective-permute-start.8 = (bf16[336,512]{1,0:T(8,128)(2,1)}, bf16[336,512]{1,0:T(8,128)(2,1)S(1)}, u32[]{:S(2)}, u32[]{:S(2)}) collective-permute-start(bf16[336,512]{1,0:T(8,128)(2,1)} %param.17), channel_id=1, source_target_pairs={{0,1},{1,2},{2,3},{3,4},{4,5},{5,6},{6,7},{7,0},{8,9},{9,10},{10,1... | collective-permute-start | bytes 1032200 | tf_op jit(solution)/shard_map/ppermute | solution.py:95
  11.8 243.4 %reduce-scatter.2.cloned.1.call-start = ((), (), s32[]{:S(2)}) async-start(), calls=%async_computation.4 | async-start | bytes 3440640 | tf_op jit(solution)/shard_map/reduce_scatter | solution.py:145
  54.4 10.0 %collective-permute-start.9 = (bf16[336,512]{1,0:T(8,128)(2,1)S(1)}, bf16[336,512]{1,0:T(8,128)(2,1)S(1)}, u32[]{:S(2)}, u32[]{:S(2)}) collective-permute-start(bf16[336,512]{1,0:T(8,128)(2,1)S(1)} %collective-permute-done.8), channel_id=1, source_target_pairs={{0,1},{1,2},{2,3},{3,4},{4,5},{5,6},{6,7},{7,0},{8,9},{9,10},{10,1... | collective-permute-start | bytes 1032200 | tf_op jit(solution)/shard_map/ppermute | solution.py:95
  64.4 14.7 %collective-permute-start.10 = (bf16[336,512]{1,0:T(8,128)(2,1)S(1)}, bf16[336,512]{1,0:T(8,128)(2,1)S(1)}, u32[]{:S(2)}, u32[]{:S(2)}) collective-permute-start(bf16[336,512]{1,0:T(8,128)(2,1)S(1)} %collective-permute-done.9), channel_id=1, source_target_pairs={{0,1},{1,2},{2,3},{3,4},{4,5},{5,6},{6,7},{7,0},{8,9},{9,10},{10,1... | collective-permute-start | bytes 1032200 | tf_op jit(solution)/shard_map/ppermute | solution.py:95
  79.1 10.6 %copy-start.2 = (bf16[336,512]{1,0:T(8,128)(2,1)}, bf16[336,512]{1,0:T(8,128)(2,1)S(1)}, u32[]{:S(2)}) copy-start(bf16[336,512]{1,0:T(8,128)(2,1)S(1)} %collective-permute-done.10) | copy-start | bytes 1032196
  79.1 10.1 %collective-permute-start.11 = (bf16[336,512]{1,0:T(8,128)(2,1)S(1)}, bf16[336,512]{1,0:T(8,128)(2,1)}, u32[]{:S(2)}, u32[]{:S(2)}) collective-permute-start(bf16[336,512]{1,0:T(8,128)(2,1)S(1)} %collective-permute-done.10), channel_id=1, source_target_pairs={{0,1},{1,2},{2,3},{3,4},{4,5},{5,6},{6,7},{7,0},{8,9},{9,10},{10,1... | collective-permute-start | bytes 1032200 | tf_op jit(solution)/shard_map/ppermute | solution.py:95
  89.1 17.3 %collective-permute-start.12 = (bf16[336,512]{1,0:T(8,128)(2,1)}, bf16[336,512]{1,0:T(8,128)(2,1)}, u32[]{:S(2)}, u32[]{:S(2)}) collective-permute-start(bf16[336,512]{1,0:T(8,128)(2,1)} %collective-permute-done.11), channel_id=1, source_target_pairs={{0,1},{1,2},{2,3},{3,4},{4,5},{5,6},{6,7},{7,0},{8,9},{9,10},{10,1... | collective-permute-start | bytes 1032200 | tf_op jit(solution)/shard_map/ppermute | solution.py:95
  106.4 13.8 %collective-permute-start.13 = (bf16[336,512]{1,0:T(8,128)(2,1)}, bf16[336,512]{1,0:T(8,128)(2,1)}, u32[]{:S(2)}, u32[]{:S(2)}) collective-permute-start(bf16[336,512]{1,0:T(8,128)(2,1)} %collective-permute-done.12), channel_id=1, source_target_pairs={{0,1},{1,2},{2,3},{3,4},{4,5},{5,6},{6,7},{7,0},{8,9},{9,10},{10,1... | collective-permute-start | bytes 1032200 | tf_op jit(solution)/shard_map/ppermute | solution.py:95
  120.2 28.3 %collective-permute-start.14 = (bf16[336,512]{1,0:T(8,128)(2,1)}, bf16[336,512]{1,0:T(8,128)(2,1)}, u32[]{:S(2)}, u32[]{:S(2)}) collective-permute-start(bf16[336,512]{1,0:T(8,128)(2,1)} %collective-permute-done.13), channel_id=1, source_target_pairs={{0,1},{1,2},{2,3},{3,4},{4,5},{5,6},{6,7},{7,0},{8,9},{9,10},{10,1... | collective-permute-start | bytes 1032200 | tf_op jit(solution)/shard_map/ppermute | solution.py:95
  120.2 4.9 %copy-start.9 = (f32[128]{0:T(128)S(1)}, f32[128]{0:T(128)}, u32[]{:S(2)}) copy-start(f32[128]{0:T(128)} %param.21) | copy-start | bytes 1540
  122.8 2.5 copy-start.6
  133.8 20.6 %copy-start.3 = (bf16[336,512]{1,0:T(8,128)(2,1)S(1)}, bf16[336,512]{1,0:T(8,128)(2,1)}, u32[]{:S(2)}) copy-start(bf16[336,512]{1,0:T(8,128)(2,1)} %copy-done.2) | copy-start | bytes 1032196
  135.6 19.0 %copy-start.1 = (bf16[336,512]{1,0:T(8,128)(2,1)S(1)}, bf16[336,512]{1,0:T(8,128)(2,1)}, u32[]{:S(2)}) copy-start(bf16[336,512]{1,0:T(8,128)(2,1)} %param.17) | copy-start | bytes 1032196
  135.6 34.1 %collective-permute-start = (bf16[2,128,512]{1,2,0:T(8,128)(2,1)}, bf16[2,128,512]{1,2,0:T(8,128)(2,1)}, u32[]{:S(2)}, u32[]{:S(2)}) collective-permute-start(bf16[2,128,512]{1,2,0:T(8,128)(2,1)} %pad_maximum_fusion), channel_id=1, source_target_pairs={} | collective-permute-start | bytes 786440 | tf_op jit(solution)/shard_map/ppermute | solution.py:17
  137.1 34.9 %collective-permute-start.1 = (bf16[2,128,512]{1,2,0:T(8,128)(2,1)}, bf16[2,128,512]{1,2,0:T(8,128)(2,1)}, u32[]{:S(2)}, u32[]{:S(2)}) collective-permute-start(bf16[2,128,512]{1,2,0:T(8,128)(2,1)} %pad_maximum_fusion), channel_id=1, source_target_pairs={{0,7},{8,15},{16,23},{24,31}} | collective-permute-start | bytes 786440 | tf_op jit(solution)/shard_map/ppermute | solution.py:17
  144.4 29.9 %collective-permute-start.2 = (bf16[2,128,512]{1,2,0:T(8,128)(2,1)}, bf16[2,128,512]{1,2,0:T(8,128)(2,1)}, u32[]{:S(2)}, u32[]{:S(2)}) collective-permute-start(bf16[2,128,512]{1,2,0:T(8,128)(2,1)} %pad_maximum_fusion), channel_id=1, source_target_pairs={{0,6},{1,7},{8,14},{9,15},{16,22},{17,23},{24,30},{25,31}} | collective-permute-start | bytes 786440 | tf_op jit(solution)/shard_map/ppermute | solution.py:17
  146.5 31.2 %collective-permute-start.3 = (bf16[2,128,512]{1,2,0:T(8,128)(2,1)}, bf16[2,128,512]{1,2,0:T(8,128)(2,1)}, u32[]{:S(2)}, u32[]{:S(2)}) collective-permute-start(bf16[2,128,512]{1,2,0:T(8,128)(2,1)} %pad_maximum_fusion), channel_id=1, source_target_pairs={{0,5},{1,6},{2,7},{8,13},{9,14},{10,15},{16,21},{17,22},{18,23},{2... | collective-permute-start | bytes 786440 | tf_op jit(solution)/shard_map/ppermute | solution.py:17
  148.5 30.3 %collective-permute-start.4 = (bf16[2,128,512]{1,2,0:T(8,128)(2,1)}, bf16[2,128,512]{1,2,0:T(8,128)(2,1)}, u32[]{:S(2)}, u32[]{:S(2)}) collective-permute-start(bf16[2,128,512]{1,2,0:T(8,128)(2,1)} %pad_maximum_fusion), channel_id=1, source_target_pairs={{0,4},{1,5},{2,6},{3,7},{8,12},{9,13},{10,14},{11,15},{16,20},{17,... | collective-permute-start | bytes 786440 | tf_op jit(solution)/shard_map/ppermute | solution.py:17
  165.5 3.2 %copy-start.10 = (f32[128]{0:T(128)S(1)}, f32[128]{0:T(128)}, u32[]{:S(2)}) copy-start(f32[128]{0:T(128)} %param.20) | copy-start | bytes 1540
  165.5 3.3 %copy-start.7 = (f32[256,64]{0,1:T(8,128)S(1)}, f32[256,64]{0,1:T(8,128)}, u32[]{:S(2)}) copy-start(f32[256,64]{0,1:T(8,128)} %get-tuple-element.19) | copy-start | bytes 196612
  168.9 20.6 %copy-start.4 = (bf16[2,128,256]{1,2,0:T(8,128)(2,1)S(1)}, bf16[2,128,256]{1,2,0:T(8,128)(2,1)}, u32[]{:S(2)}) copy-start(bf16[2,128,256]{1,2,0:T(8,128)(2,1)} %copy.25) | copy-start | bytes 393220
  168.9 20.6 %copy-start.5 = (bf16[2,128,256]{1,2,0:T(8,128)(2,1)S(1)}, bf16[2,128,256]{1,2,0:T(8,128)(2,1)}, u32[]{:S(2)}) copy-start(bf16[2,128,256]{1,2,0:T(8,128)(2,1)} %copy.26) | copy-start | bytes 393220
  169.7 11.2 %collective-permute-start.5 = (bf16[2,128,512]{1,2,0:T(8,128)(2,1)}, bf16[2,128,512]{1,2,0:T(8,128)(2,1)S(1)}, u32[]{:S(2)}, u32[]{:S(2)}) collective-permute-start(bf16[2,128,512]{1,2,0:T(8,128)(2,1)} %pad_maximum_fusion), channel_id=1, source_target_pairs={{0,3},{1,4},{2,5},{3,6},{4,7},{8,11},{9,12},{10,13},{11,14},{12,15... | collective-permute-start | bytes 786440 | tf_op jit(solution)/shard_map/ppermute | solution.py:17
  172.0 17.3 %collective-permute-start.6 = (bf16[2,128,512]{1,2,0:T(8,128)(2,1)}, bf16[2,128,512]{1,2,0:T(8,128)(2,1)S(1)}, u32[]{:S(2)}, u32[]{:S(2)}) collective-permute-start(bf16[2,128,512]{1,2,0:T(8,128)(2,1)} %pad_maximum_fusion), channel_id=1, source_target_pairs={{0,2},{1,3},{2,4},{3,5},{4,6},{5,7},{8,10},{9,11},{10,12},{11,13},... | collective-permute-start | bytes 786440 | tf_op jit(solution)/shard_map/ppermute | solution.py:17
  174.4 15.1 %collective-permute-start.7 = (bf16[2,128,512]{1,2,0:T(8,128)(2,1)}, bf16[2,128,512]{1,2,0:T(8,128)(2,1)S(1)}, u32[]{:S(2)}, u32[]{:S(2)}) collective-permute-start(bf16[2,128,512]{1,2,0:T(8,128)(2,1)} %pad_maximum_fusion), channel_id=1, source_target_pairs={{0,1},{1,2},{2,3},{3,4},{4,5},{5,6},{6,7},{8,9},{9,10},{10,11},{11... | collective-permute-start | bytes 786440 | tf_op jit(solution)/shard_map/ppermute | solution.py:17
  189.6 1.3 copy-start.8
  205.2 70.5 %copy-start.11 = (s32[2]{0:T(128)S(1)}, s32[2]{0:T(128)}, u32[]{:S(2)}) copy-start(s32[2]{0:T(128)} %param.15) | copy-start | bytes 28
  205.2 70.5 %copy-start.12 = (s32[2]{0:T(128)S(1)}, s32[2]{0:T(128)}, u32[]{:S(2)}) copy-start(s32[2]{0:T(128)} %param.14) | copy-start | bytes 28
Sparse Core Ops, SparseCore 0:
  10.2 46.6 all-gather.3
  59.1 52.0 all-gather.5
  113.4 82.8 all-gather.7
  205.4 49.7 reduce-scatter.1
